TPU v7x, 256 devices: a whole 4x4x8 slice. The times are simulated.
256 devices in a mesh: sec: 64 (over y, z, core), reg: 4 (over x).
Axes of the slice: x: 4, y: 4, z: 8, core: 2. Of those that a mesh axis runs over, the one named last changes fastest.
Arguments:
- start_params: float32 [64, 4, 20, 128], P('sec', 'reg'), may hold values from -3 to 3
- right_side: float32 [64, 4, 20, 128], P('sec', 'reg'), may hold values from -40 to 40
- prior: float32 [64, 4, 20, 128], P('sec', 'reg'), may hold values from 0.1 to 1
- matches: bfloat16 [64, 4, 640, 4, 256], P('sec', 'reg'), may hold values from -1 to 1
- pair_first: int32 [64, 4, 640], P('sec', 'reg'), may hold values from 0 to 127, as said below
- pair_second: int32 [64, 4, 640], P('sec', 'reg'), may hold values from 0 to 415, as said below
- match_counts: int32 [64, 4, 640], P('sec', 'reg'), may hold values from 0 to 256, as said below
- send_lists: int32 [64, 4, 2, 16], P('sec', 'reg'), may hold values from 0 to 127, as said below
Outputs:
- solution: float32 [64, 4, 20, 128], P('sec', 'reg')
- residual: float32 [64, 4, 20, 128], P('sec', 'reg')
Inputs may be any that keep to these rules, and one draw needn't show every extreme that they name: Each tile is pair_first of exactly five pairs of its device, in a drawn order. `pair_second`: names a column of the extended field; blocks of neighbours outside the grid are never named; a pair with match count 0 names its own tile. `match_counts`: 0 marks an absent pair; every device has a pair with exactly 256 matches. `send_lists`: row 0 holds the tiles whose coefficients a region lends to the region below it, row 1 to the region above; each row has 16 distinct tiles and the rows are disjoint.
All inputs are finite; a program needn't handle non-finite values.
Results may differ from a plain program's by a relative error of at most 0.0003.
Values sent between devices are 32-bit elements; how exact they have to be, the bound alone decides.
A program may use at most 64 MiB of HBM per device.

v0:
```python
import math
import jax
import jax.numpy as jnp
from jax import lax
from jax.sharding import PartitionSpec as P

FULL_PRECISION = lax.Precision.HIGHEST


def shifted(array, axis, by):
    length = lax.axis_size(axis)
    pairs = [(i, i + by) for i in range(length) if 0 <= i + by < length]
    return lax.ppermute(array, axis, pairs)


def padded_2(array, sides, width):
    for axis, dim in sides:
        size, length = (lax.axis_size(axis), array.shape[dim])
        up = [(i, (i + 1) % size) for i in range(size - 1)]
        down = [(j, i) for i, j in up]
        last = lax.slice_in_dim(array, length - width, length, axis=dim)
        first = lax.slice_in_dim(array, 0, width, axis=dim)
        before = lax.ppermute(last, axis, up)
        after = lax.ppermute(first, axis, down)
        array = jnp.concatenate([before, array, after], axis=dim)
    return array


def monomials(across, upward):
    constant = jnp.ones_like(across)
    square_a = across * across
    square_b = upward * upward
    mixed = across * upward
    return jnp.stack(
        [
            constant,
            across,
            upward,
            square_a,
            mixed,
            square_b,
            square_a * across,
            square_a * upward,
            square_b * across,
            square_b * upward,
        ]
    )


def match_bases(count_blk, match_blk):
    points = match_blk.astype(jnp.float32)
    slots = points.shape[-1]
    basis_a = monomials(points[:, 0], points[:, 1])
    basis_b = monomials(points[:, 2], points[:, 3])
    weights = jnp.where(jnp.arange(slots)[None, :] < count_blk[:, None], 2.0 / slots, 0.0).astype(
        jnp.float32
    )
    return (basis_a, basis_b, weights)


def block_terms(extended, first_blk, second_blk, count_blk, match_blk):
    width = first_blk.shape[0]
    basis_a, basis_b, weights = match_bases(count_blk, match_blk)
    own = jnp.take(extended, first_blk, axis=1).reshape(2, 10, width)
    other = jnp.take(extended, second_blk, axis=1).reshape(2, 10, width)
    mismatch = (
        jnp.einsum("mpk,cmp->cpk", basis_a, own, precision=FULL_PRECISION)
        - jnp.einsum("mpk,cmp->cpk", basis_b, other, precision=FULL_PRECISION)
    ) * weights[None]
    to_own = jnp.einsum("mpk,cpk->cmp", basis_a, mismatch, precision=FULL_PRECISION).reshape(
        20, width
    )
    to_other = -jnp.einsum("mpk,cpk->cmp", basis_b, mismatch, precision=FULL_PRECISION).reshape(
        20, width
    )
    return (to_own, to_other)


def split_blocks(first, second, counts, matches):
    pairs = first.shape[0]
    block = math.gcd(pairs, 512)
    blocks = pairs // block
    slots = matches.shape[-1]
    return (
        first.reshape(blocks, block),
        second.reshape(blocks, block),
        counts.reshape(blocks, block),
        matches.reshape(blocks, block, 4, slots),
    )


def extend(params, send_lists):
    arrived = params
    taken = []
    for hop_index in range(2):
        arrived = shifted(arrived, "sec", 1)
        taken.append(arrived)
    near_params, far_params = (taken[0], taken[1])
    faces = jnp.stack(
        [jnp.take(params, send_lists[0], axis=1), jnp.take(params, send_lists[1], axis=1)]
    )
    padded = padded_2(faces, (("reg", 0),), 1)
    return jnp.concatenate([params, near_params, far_params, padded[0], padded[3]], axis=1)


def fold_back(products, tiles, rows, send_lists):
    local = products[:, :tiles]
    near_part = products[:, tiles : 2 * tiles]
    far_part = products[:, 2 * tiles : 3 * tiles]
    outgoing = far_part
    arrived = far_part
    for hop_index in range(2):
        arrived = shifted(outgoing, "sec", -1)
        outgoing = near_part + arrived
    local = local + arrived
    faces = jnp.stack([products[:, 3 * tiles : 3 * tiles + rows], products[:, 3 * tiles + rows :]])
    padded = padded_2(faces, (("reg", 0),), 1)
    local = local.at[:, send_lists[0]].add(padded[0])
    return local.at[:, send_lists[1]].add(padded[3])


def apply_normal(params, prior, first, second, counts, matches, send_lists):
    tiles = params.shape[1]
    rows = send_lists.shape[1]
    pairs = first.shape[0]
    extended = extend(params, send_lists)
    pieces = split_blocks(first, second, counts, matches)
    to_own, to_other = lax.map(
        lambda items: block_terms(extended, items[0], items[1], items[2], items[3]), pieces
    )
    to_own = jnp.moveaxis(to_own, 0, 1).reshape(20, pairs)
    to_other = jnp.moveaxis(to_other, 0, 1).reshape(20, pairs)
    products = jnp.zeros((20, extended.shape[1]), jnp.float32)
    products = products.at[:, first].add(to_own).at[:, second].add(to_other)
    return fold_back(products, tiles, rows, send_lists) + prior * params


def global_dot(value):
    return lax.psum(value, ("sec", "reg"))


def on_device(
    start_params, right_side, prior, matches, pair_first, pair_second, match_counts, send_lists
):
    params_start = start_params[0, 0]
    target = right_side[0, 0]
    damping = prior[0, 0]
    first = pair_first[0, 0]
    second = pair_second[0, 0]
    counts = match_counts[0, 0]
    points = matches[0, 0]
    border = send_lists[0, 0]

    def normal(field):
        return apply_normal(field, damping, first, second, counts, points, border)

    solution = params_start
    residual = target - normal(params_start)
    direction = residual
    norm_now = global_dot(jnp.sum(residual * residual))
    image = normal(direction)
    alpha = norm_now / global_dot(jnp.sum(direction * image))
    solution = solution + alpha * direction
    residual = residual - alpha * image
    return (solution[None, None], residual[None, None])


def solution(mesh):
    return jax.shard_map(
        on_device,
        mesh=mesh,
        in_specs=(
            P("sec", "reg", None, None),
            P("sec", "reg", None, None),
            P("sec", "reg", None, None),
            P("sec", "reg", None, None, None),
            P("sec", "reg", None),
            P("sec", "reg", None),
            P("sec", "reg", None),
            P("sec", "reg", None, None),
        ),
        out_specs=(P("sec", "reg", None, None), P("sec", "reg", None, None)),
        check_vma=False,
    )
```

profile of v0, /device:TPU:1, one launch (start us, length us, event | category | flops | bytes accessed | tf_op | source)
XLA Modules:
  0.0 497.0 jit_solution(6133939188612458602)
XLA Ops:
  1.4 4.9 collective-permute-start
  7.8 3.1 collective-permute-start.2
  14.2 2.2 collective-permute-start.1
  23.0 152.0 %while.24 = (s32[]{:T(128)}, f32[5,20,128]{2,1,0:T(8,128)}, f32[5,20,128]{2,1,0:T(8,128)}, s32[5,128]{1,0:T(8,128)S(1)}, f32[20,416]{0,1:T(8,128)}, /*index=5*/b...) while((s32[]{:T(128)}, f32[5,20,128]{2,1,0:T(8,128)}, ...), condition=%wide.region_1.4_spmd, body=%wide.region_0.3_spmd.sunk | while | flops 32287744 | bytes 16952436 | solution.py:128
  24.0 1.9 multiply_multiply_fusion.20
  27.2 4.8 stack.53
  32.7 5.4 %stack.52 = f32[10,128,256]{2,0,1:T(8,128)} concatenate(f32[1,128,256]{2,0,1:T(1,128)S(1)} %broadcast.300, f32[1,128,256]{2,0,1:T(1,128)} %get-tuple-element.348, f32[1,128,256]{2,0,1:T(1,128)} %get-tuple-element.349, f32[1,128,256]{2,0,1:T(1,128)S(1)} %get-tuple-element.350, f32[1,128,256]{2,0,1:T(1,128)S(1)} %get-tuple-element.351, f32[1,128,256]{2,0,1:T(1,128)S(1)} %get-tuple-element.352, ...), dimensions={0} | concatenate | bytes 2621440 | tf_op jit(solution)/shard_map/while/body/eval_jaxpr/stack | solution.py:34
  40.0 2.8 fusion.96
  49.3 3.4 convolution_bitcast_fusion.4
  57.6 4.8 stack.53
  63.1 5.4 %stack.52 = f32[10,128,256]{2,0,1:T(8,128)} concatenate(f32[1,128,256]{2,0,1:T(1,128)S(1)} %broadcast.300, f32[1,128,256]{2,0,1:T(1,128)} %get-tuple-element.348, f32[1,128,256]{2,0,1:T(1,128)} %get-tuple-element.349, f32[1,128,256]{2,0,1:T(1,128)S(1)} %get-tuple-element.350, f32[1,128,256]{2,0,1:T(1,128)S(1)} %get-tuple-element.351, f32[1,128,256]{2,0,1:T(1,128)S(1)} %get-tuple-element.352, ...), dimensions={0} | concatenate | bytes 2621440 | tf_op jit(solution)/shard_map/while/body/eval_jaxpr/stack | solution.py:34
  70.4 2.8 fusion.96
  79.7 3.4 convolution_bitcast_fusion.4
  87.9 4.8 stack.53
  93.5 5.4 %stack.52 = f32[10,128,256]{2,0,1:T(8,128)} concatenate(f32[1,128,256]{2,0,1:T(1,128)S(1)} %broadcast.300, f32[1,128,256]{2,0,1:T(1,128)} %get-tuple-element.348, f32[1,128,256]{2,0,1:T(1,128)} %get-tuple-element.349, f32[1,128,256]{2,0,1:T(1,128)S(1)} %get-tuple-element.350, f32[1,128,256]{2,0,1:T(1,128)S(1)} %get-tuple-element.351, f32[1,128,256]{2,0,1:T(1,128)S(1)} %get-tuple-element.352, ...), dimensions={0} | concatenate | bytes 2621440 | tf_op jit(solution)/shard_map/while/body/eval_jaxpr/stack | solution.py:34
  100.8 2.8 fusion.96
  110.0 3.4 convolution_bitcast_fusion.4
  115.2 1.9 multiply_multiply_fusion.20
  118.3 4.8 stack.53
  123.9 5.4 %stack.52 = f32[10,128,256]{2,0,1:T(8,128)} concatenate(f32[1,128,256]{2,0,1:T(1,128)S(1)} %broadcast.300, f32[1,128,256]{2,0,1:T(1,128)} %get-tuple-element.348, f32[1,128,256]{2,0,1:T(1,128)} %get-tuple-element.349, f32[1,128,256]{2,0,1:T(1,128)S(1)} %get-tuple-element.350, f32[1,128,256]{2,0,1:T(1,128)S(1)} %get-tuple-element.351, f32[1,128,256]{2,0,1:T(1,128)S(1)} %get-tuple-element.352, ...), dimensions={0} | concatenate | bytes 2621440 | tf_op jit(solution)/shard_map/while/body/eval_jaxpr/stack | solution.py:34
  131.2 2.8 fusion.96
  140.5 3.4 convolution_bitcast_fusion.4
  148.7 4.8 stack.53
  154.3 5.4 %stack.52 = f32[10,128,256]{2,0,1:T(8,128)} concatenate(f32[1,128,256]{2,0,1:T(1,128)S(1)} %broadcast.300, f32[1,128,256]{2,0,1:T(1,128)} %get-tuple-element.348, f32[1,128,256]{2,0,1:T(1,128)} %get-tuple-element.349, f32[1,128,256]{2,0,1:T(1,128)S(1)} %get-tuple-element.350, f32[1,128,256]{2,0,1:T(1,128)S(1)} %get-tuple-element.351, f32[1,128,256]{2,0,1:T(1,128)S(1)} %get-tuple-element.352, ...), dimensions={0} | concatenate | bytes 2621440 | tf_op jit(solution)/shard_map/while/body/eval_jaxpr/stack | solution.py:34
  161.6 2.8 fusion.96
  170.8 3.4 convolution_bitcast_fusion.4
  177.2 6.4 %scatter_custom_fusion = f32[20,416]{0,1:T(8,128)S(1)} fusion(s32[640]{0:T(1024)} %fusion.40, f32[640,20]{1,0:T(8,128)S(1)} %copy.78, f32[]{:T(128)} %constant.56.clone.1), kind=kCustom, calls=%fused_computation.104 | custom fusion | flops 12800 | bytes 33792 | tf_op jit(solution)/shard_map/scatter-add | solution.py:134
  183.6 6.1 %scatter_fusion = f32[20,416]{0,1:T(8,128)S(1)} fusion(f32[20,416]{0,1:T(8,128)S(1)} %scatter_custom_fusion, s32[640]{0:T(1024)S(1)} %fusion.41, f32[640,20]{1,0:T(8,128)S(1)} %copy.80), kind=kCustom, calls=%fused_computation.9 | custom fusion | flops 12800 | bytes 156160 | tf_op jit(solution)/shard_map/scatter-add | solution.py:134
  189.7 2.1 collective-permute-start.4
  192.1 3.2 collective-permute-done.4
  197.2 4.3 collective-permute-start.6
  203.6 2.3 collective-permute-done.7
  206.6 5.1 %collective-permute-start.8 = (f32[20,128]{0,1:T(8,128)S(1)}, f32[20,128]{0,1:T(8,128)S(1)}, u32[]{:S(2)}, u32[]{:S(2)}) collective-permute-start(f32[20,128]{0,1:T(8,128)S(1)} %bitcast_subtract_fusion), channel_id=1, source_target_pairs={{0,4},{4,8},{8,12},{12,16},{16,20},{20,24},{24,28},{28,32},{32,36}... | collective-permute-start | bytes 30728 | tf_op jit(solution)/shard_map/ppermute | solution.py:13
  213.0 3.1 collective-permute-start.10
  216.2 2.2 collective-permute-start.9
  219.9 2.9 collective-permute-done.11
  225.3 152.0 %while.25 = (s32[]{:T(128)}, f32[5,20,128]{2,1,0:T(8,128)}, f32[5,20,128]{2,1,0:T(8,128)}, s32[5,128]{1,0:T(8,128)S(1)}, f32[20,416]{0,1:T(8,128)}, /*index=5*/b...) while((s32[]{:T(128)}, f32[5,20,128]{2,1,0:T(8,128)}, ...), condition=%wide.region_9.12_spmd, body=%wide.region_8.11_spmd.sunk | while | flops 32287744 | bytes 16952436 | solution.py:128
  229.5 4.8 stack.71
  235.1 5.4 %stack.70 = f32[10,128,256]{2,0,1:T(8,128)} concatenate(f32[1,128,256]{2,0,1:T(1,128)S(1)} %broadcast.309, f32[1,128,256]{2,0,1:T(1,128)} %get-tuple-element.377, f32[1,128,256]{2,0,1:T(1,128)} %get-tuple-element.378, f32[1,128,256]{2,0,1:T(1,128)S(1)} %get-tuple-element.379, f32[1,128,256]{2,0,1:T(1,128)S(1)} %get-tuple-element.380, f32[1,128,256]{2,0,1:T(1,128)S(1)} %get-tuple-element.381, ...), dimensions={0} | concatenate | bytes 2621440 | tf_op jit(solution)/shard_map/while/body/eval_jaxpr/stack | solution.py:34
  242.3 2.8 fusion.109
  251.6 3.4 convolution_bitcast_fusion.5
  259.9 4.8 stack.71
  265.5 5.4 %stack.70 = f32[10,128,256]{2,0,1:T(8,128)} concatenate(f32[1,128,256]{2,0,1:T(1,128)S(1)} %broadcast.309, f32[1,128,256]{2,0,1:T(1,128)} %get-tuple-element.377, f32[1,128,256]{2,0,1:T(1,128)} %get-tuple-element.378, f32[1,128,256]{2,0,1:T(1,128)S(1)} %get-tuple-element.379, f32[1,128,256]{2,0,1:T(1,128)S(1)} %get-tuple-element.380, f32[1,128,256]{2,0,1:T(1,128)S(1)} %get-tuple-element.381, ...), dimensions={0} | concatenate | bytes 2621440 | tf_op jit(solution)/shard_map/while/body/eval_jaxpr/stack | solution.py:34
  272.7 2.8 fusion.109
  282.0 3.4 convolution_bitcast_fusion.5
  290.3 4.8 stack.71
  295.9 5.4 %stack.70 = f32[10,128,256]{2,0,1:T(8,128)} concatenate(f32[1,128,256]{2,0,1:T(1,128)S(1)} %broadcast.309, f32[1,128,256]{2,0,1:T(1,128)} %get-tuple-element.377, f32[1,128,256]{2,0,1:T(1,128)} %get-tuple-element.378, f32[1,128,256]{2,0,1:T(1,128)S(1)} %get-tuple-element.379, f32[1,128,256]{2,0,1:T(1,128)S(1)} %get-tuple-element.380, f32[1,128,256]{2,0,1:T(1,128)S(1)} %get-tuple-element.381, ...), dimensions={0} | concatenate | bytes 2621440 | tf_op jit(solution)/shard_map/while/body/eval_jaxpr/stack | solution.py:34
  303.1 2.8 fusion.109
  312.4 3.4 convolution_bitcast_fusion.5
  320.7 4.8 stack.71
  326.2 5.4 %stack.70 = f32[10,128,256]{2,0,1:T(8,128)} concatenate(f32[1,128,256]{2,0,1:T(1,128)S(1)} %broadcast.309, f32[1,128,256]{2,0,1:T(1,128)} %get-tuple-element.377, f32[1,128,256]{2,0,1:T(1,128)} %get-tuple-element.378, f32[1,128,256]{2,0,1:T(1,128)S(1)} %get-tuple-element.379, f32[1,128,256]{2,0,1:T(1,128)S(1)} %get-tuple-element.380, f32[1,128,256]{2,0,1:T(1,128)S(1)} %get-tuple-element.381, ...), dimensions={0} | concatenate | bytes 2621440 | tf_op jit(solution)/shard_map/while/body/eval_jaxpr/stack | solution.py:34
  333.5 2.8 fusion.109
  342.8 3.4 convolution_bitcast_fusion.5
  351.0 4.8 stack.71
  356.6 5.4 %stack.70 = f32[10,128,256]{2,0,1:T(8,128)} concatenate(f32[1,128,256]{2,0,1:T(1,128)S(1)} %broadcast.309, f32[1,128,256]{2,0,1:T(1,128)} %get-tuple-element.377, f32[1,128,256]{2,0,1:T(1,128)} %get-tuple-element.378, f32[1,128,256]{2,0,1:T(1,128)S(1)} %get-tuple-element.379, f32[1,128,256]{2,0,1:T(1,128)S(1)} %get-tuple-element.380, f32[1,128,256]{2,0,1:T(1,128)S(1)} %get-tuple-element.381, ...), dimensions={0} | concatenate | bytes 2621440 | tf_op jit(solution)/shard_map/while/body/eval_jaxpr/stack | solution.py:34
  363.9 2.8 fusion.109
  373.2 3.4 convolution_bitcast_fusion.5
  379.5 6.4 %scatter_custom_fusion.4 = f32[20,416]{0,1:T(8,128)S(1)} fusion(s32[640]{0:T(1024)} %fusion.40, f32[640,20]{1,0:T(8,128)S(1)} %copy.89, f32[]{:T(128)} %constant.56.clone.1), kind=kCustom, calls=%fused_computation.102 | custom fusion | flops 12800 | bytes 33792 | tf_op jit(solution)/shard_map/scatter-add | solution.py:134
  385.9 6.1 %scatter_fusion.1 = f32[20,416]{0,1:T(8,128)S(1)} fusion(f32[20,416]{0,1:T(8,128)S(1)} %scatter_custom_fusion.4, s32[640]{0:T(1024)S(1)} %fusion.41, f32[640,20]{1,0:T(8,128)S(1)} %copy.91), kind=kCustom, calls=%fused_computation.13 | custom fusion | flops 12800 | bytes 156160 | tf_op jit(solution)/shard_map/scatter-add | solution.py:134
  392.0 3.3 collective-permute-start.12
  395.3 3.5 collective-permute-done.12
  400.8 2.8 collective-permute-start.14
  405.8 2.2 collective-permute-done.15
  409.4 84.8 %all-reduce = (f32[]{:T(128)}, f32[]{:T(128)}) all-reduce(f32[]{:T(128)} %get-tuple-element.119, f32[]{:T(128)} %get-tuple-element.118), channel_id=1, replica_groups=mesh['sec'=64,'reg'=4] {'sec','reg'}, use_global_device_ids=true, to_apply=%region_7.10 | all-reduce | flops 2 | bytes 16 | tf_op jit(solution)/shard_map/psum | solution.py:139
  (360 shorter events, 168.1 us)
Async XLA Ops:
  1.4 21.6 %copy-start.2 = (f32[1,1,20,128]{2,3,1,0:T(8,128)}, f32[1,1,20,128]{2,3,1,0:T(8,128)S(1)}, u32[]{:S(2)}) copy-start(f32[1,1,20,128]{2,3,1,0:T(8,128)S(1)} %copy.69) | copy-start | bytes 30724
  1.4 12.7 %collective-permute-start = (f32[20,128]{0,1:T(8,128)S(1)}, f32[20,128]{0,1:T(8,128)S(1)}, u32[]{:S(2)}, u32[]{:S(2)}) collective-permute-start(f32[20,128]{0,1:T(8,128)S(1)} %bitcast.359), channel_id=1, source_target_pairs={{0,4},{4,8},{8,12},{12,16},{16,20},{20,24},{24,28},{28,32},{32,36}... | collective-permute-start | bytes 30728 | tf_op jit(solution)/shard_map/ppermute | solution.py:13
  7.1 3.8 copy-start.12
  7.1 13.3 %copy-start.10 = (pred[16]{0:T(512)(128)(4,1)}, pred[16]{0:T(512)(128)(4,1)S(1)}, u32[]{:S(2)}) copy-start(pred[16]{0:T(512)(128)(4,1)S(1)} %get-tuple-element.162) | copy-start | bytes 52
  7.8 12.7 %collective-permute-start.2 = (f32[1,20,16]{1,2,0:T(8,128)S(1)}, f32[1,20,16]{1,2,0:T(8,128)S(1)}, u32[]{:S(2)}, u32[]{:S(2)}) collective-permute-start(f32[1,20,16]{1,2,0:T(8,128)S(1)} %select_bitcast_fusion.7), channel_id=1, source_target_pairs={{0,1},{1,2},{2,3},{4,5},{5,6},{6,7},{8,9},{9,10},{10,11},{12,13},{... | collective-permute-start | bytes 3848 | tf_op jit(solution)/shard_map/ppermute | solution.py:23
  10.9 9.6 %copy-start.9 = (s32[1024]{0:T(1024)}, s32[1024]{0:T(1024)S(1)}, u32[]{:S(2)}) copy-start(s32[1024]{0:T(1024)S(1)} %pad_clamp_fusion.4) | copy-start | bytes 12292
  11.6 9.0 %collective-permute-start.3 = (f32[1,20,16]{1,2,0:T(8,128)S(1)}, f32[1,20,16]{1,2,0:T(8,128)S(1)}, u32[]{:S(2)}, u32[]{:S(2)}) collective-permute-start(f32[1,20,16]{1,2,0:T(8,128)S(1)} %select_bitcast_fusion.6), channel_id=1, source_target_pairs={{1,0},{2,1},{3,2},{5,4},{6,5},{7,6},{9,8},{10,9},{11,10},{13,12},{... | collective-permute-start | bytes 3848 | tf_op jit(solution)/shard_map/ppermute | solution.py:24
  14.2 6.5 %collective-permute-start.1 = (f32[20,128]{0,1:T(8,128)S(1)}, f32[20,128]{0,1:T(8,128)S(1)}, u32[]{:S(2)}, u32[]{:S(2)}) collective-permute-start(f32[20,128]{0,1:T(8,128)S(1)} %collective-permute-done), channel_id=1, source_target_pairs={{0,4},{4,8},{8,12},{12,16},{16,20},{20,24},{24,28},{28,32},{32,36}... | collective-permute-start | bytes 30728 | tf_op jit(solution)/shard_map/ppermute | solution.py:13
  175.0 16.9 %copy-start.14 = (s32[1,1,2,16]{3,2,1,0:T(2,128)S(1)}, s32[1,1,2,16]{3,2,1,0:T(2,128)}, u32[]{:S(2)}) copy-start(s32[1,1,2,16]{3,2,1,0:T(2,128)} %param.23) | copy-start | bytes 388
  175.0 16.9 %copy-start.7 = (f32[1,1,20,128]{3,1,2,0:T(1,128)S(1)}, f32[1,1,20,128]{3,1,2,0:T(1,128)}, u32[]{:S(2)}) copy-start(f32[1,1,20,128]{3,1,2,0:T(1,128)} %param.18) | copy-start | bytes 30724
  175.0 17.0 %copy-start.8 = (f32[1,1,20,128]{3,1,2,0:T(1,128)S(1)}, f32[1,1,20,128]{3,1,2,0:T(1,128)}, u32[]{:S(2)}) copy-start(f32[1,1,20,128]{3,1,2,0:T(1,128)} %param.17) | copy-start | bytes 30724
  175.0 27.8 %copy-start.3 = (f32[1,1,20,128]{2,3,1,0:T(8,128)S(1)}, f32[1,1,20,128]{2,3,1,0:T(8,128)}, u32[]{:S(2)}) copy-start(f32[1,1,20,128]{2,3,1,0:T(8,128)} %copy-done.2) | copy-start | bytes 30724
  175.9 36.4 %copy-start.13 = (pred[16]{0:T(512)(128)(4,1)S(1)}, pred[16]{0:T(512)(128)(4,1)}, u32[]{:S(2)}) copy-start(pred[16]{0:T(512)(128)(4,1)} %copy-done.12) | copy-start | bytes 52
  175.9 42.5 %copy-start.11 = (pred[16]{0:T(512)(128)(4,1)S(1)}, pred[16]{0:T(512)(128)(4,1)}, u32[]{:S(2)}) copy-start(pred[16]{0:T(512)(128)(4,1)} %copy-done.10) | copy-start | bytes 52
  189.7 5.6 %collective-permute-start.4 = (f32[20,128]{0,1:T(8,128)S(1)}, f32[20,128]{0,1:T(8,128)S(1)}, u32[]{:S(2)}, u32[]{:S(2)}) collective-permute-start(f32[20,128]{0,1:T(8,128)S(1)} %slice.106), channel_id=1, source_target_pairs={{4,0},{8,4},{12,8},{16,12},{20,16},{24,20},{28,24},{32,28},{36,32}... | collective-permute-start | bytes 30728 | tf_op jit(solution)/shard_map/ppermute | solution.py:13
  191.9 33.4 %copy-start.15 = (s32[16]{0:T(128)}, s32[16]{0:T(128)S(1)}, u32[]{:S(2)}) copy-start(s32[16]{0:T(128)S(1)} %get-tuple-element.210) | copy-start | bytes 196
  191.9 33.4 %copy-start.16 = (s32[16]{0:T(128)}, s32[16]{0:T(128)S(1)}, u32[]{:S(2)}) copy-start(s32[16]{0:T(128)S(1)} %get-tuple-element.211) | copy-start | bytes 196
  192.0 33.3 %copy-start.5 = (f32[1,1,20,128]{2,3,1,0:T(8,128)}, f32[1,1,20,128]{2,3,1,0:T(8,128)S(1)}, u32[]{:S(2)}) copy-start(f32[1,1,20,128]{2,3,1,0:T(8,128)S(1)} %copy.81) | copy-start | bytes 30724
  195.3 7.5 %collective-permute-start.5 = (f32[20,128]{0,1:T(8,128)S(1)}, f32[20,128]{0,1:T(8,128)S(1)}, u32[]{:S(2)}, u32[]{:S(2)}) collective-permute-start(f32[20,128]{0,1:T(8,128)S(1)} %slice_add_fusion.2), channel_id=1, source_target_pairs={{4,0},{8,4},{12,8},{16,12},{20,16},{24,20},{28,24},{32,28},{36,32}... | collective-permute-start | bytes 30728 | tf_op jit(solution)/shard_map/ppermute | solution.py:13
  197.2 5.6 %collective-permute-start.6 = (f32[1,20,16]{1,2,0:T(8,128)S(1)}, f32[1,20,16]{1,2,0:T(8,128)S(1)}, u32[]{:S(2)}, u32[]{:S(2)}) collective-permute-start(f32[1,20,16]{1,2,0:T(8,128)S(1)} %get-tuple-element.207), channel_id=1, source_target_pairs={{0,1},{1,2},{2,3},{4,5},{5,6},{6,7},{8,9},{9,10},{10,11},{12,13},{... | collective-permute-start | bytes 3848 | tf_op jit(solution)/shard_map/ppermute | solution.py:23
  201.5 4.4 collective-permute-start.7
  206.6 18.7 %copy-start = (f32[20,128]{0,1:T(8,128)}, f32[20,128]{0,1:T(8,128)S(1)}, u32[]{:S(2)}) copy-start(f32[20,128]{0,1:T(8,128)S(1)} %bitcast_subtract_fusion) | copy-start | bytes 30724
  206.6 9.5 %collective-permute-start.8 = (f32[20,128]{0,1:T(8,128)S(1)}, f32[20,128]{0,1:T(8,128)S(1)}, u32[]{:S(2)}, u32[]{:S(2)}) collective-permute-start(f32[20,128]{0,1:T(8,128)S(1)} %bitcast_subtract_fusion), channel_id=1, source_target_pairs={{0,4},{4,8},{8,12},{12,16},{16,20},{20,24},{24,28},{28,32},{32,36}... | collective-permute-start | bytes 30728 | tf_op jit(solution)/shard_map/ppermute | solution.py:13
  213.0 6.8 %collective-permute-start.10 = (f32[1,20,16]{1,2,0:T(8,128)S(1)}, f32[1,20,16]{1,2,0:T(8,128)S(1)}, u32[]{:S(2)}, u32[]{:S(2)}) collective-permute-start(f32[1,20,16]{1,2,0:T(8,128)S(1)} %select_bitcast_fusion.5), channel_id=1, source_target_pairs={{0,1},{1,2},{2,3},{4,5},{5,6},{6,7},{8,9},{9,10},{10,11},{12,13},{... | collective-permute-start | bytes 3848 | tf_op jit(solution)/shard_map/ppermute | solution.py:23
  216.2 6.8 %collective-permute-start.9 = (f32[20,128]{0,1:T(8,128)S(1)}, f32[20,128]{0,1:T(8,128)S(1)}, u32[]{:S(2)}, u32[]{:S(2)}) collective-permute-start(f32[20,128]{0,1:T(8,128)S(1)} %collective-permute-done.8), channel_id=1, source_target_pairs={{0,4},{4,8},{8,12},{12,16},{16,20},{20,24},{24,28},{28,32},{32,36}... | collective-permute-start | bytes 30728 | tf_op jit(solution)/shard_map/ppermute | solution.py:13
  218.5 4.4 collective-permute-start.11
  377.3 27.6 %copy-start.1 = (f32[20,128]{0,1:T(8,128)S(1)}, f32[20,128]{0,1:T(8,128)}, u32[]{:S(2)}) copy-start(f32[20,128]{0,1:T(8,128)} %copy-done) | copy-start | bytes 30724
  377.3 27.6 %copy-start.6 = (f32[1,1,20,128]{2,3,1,0:T(8,128)S(1)}, f32[1,1,20,128]{2,3,1,0:T(8,128)}, u32[]{:S(2)}) copy-start(f32[1,1,20,128]{2,3,1,0:T(8,128)} %copy-done.5) | copy-start | bytes 30724
  377.3 118.3 %copy-start.4 = (f32[1,1,20,128]{2,3,1,0:T(8,128)S(1)}, f32[1,1,20,128]{2,3,1,0:T(8,128)}, u32[]{:S(2)}) copy-start(f32[1,1,20,128]{2,3,1,0:T(8,128)} %copy-done.2) | copy-start | bytes 30724
  392.0 6.8 %collective-permute-start.12 = (f32[20,128]{0,1:T(8,128)S(1)}, f32[20,128]{0,1:T(8,128)S(1)}, u32[]{:S(2)}, u32[]{:S(2)}) collective-permute-start(f32[20,128]{0,1:T(8,128)S(1)} %slice.111), channel_id=1, source_target_pairs={{4,0},{8,4},{12,8},{16,12},{20,16},{24,20},{28,24},{32,28},{36,32}... | collective-permute-start | bytes 30728 | tf_op jit(solution)/shard_map/ppermute | solution.py:13
  398.8 6.1 %collective-permute-start.13 = (f32[20,128]{0,1:T(8,128)S(1)}, f32[20,128]{0,1:T(8,128)S(1)}, u32[]{:S(2)}, u32[]{:S(2)}) collective-permute-start(f32[20,128]{0,1:T(8,128)S(1)} %slice_add_fusion), channel_id=1, source_target_pairs={{4,0},{8,4},{12,8},{16,12},{20,16},{24,20},{28,24},{32,28},{36,32}... | collective-permute-start | bytes 30728 | tf_op jit(solution)/shard_map/ppermute | solution.py:13
  400.8 4.2 collective-permute-start.14
  403.6 4.4 collective-permute-start.15
where the time goes:
time: 506 us; the launch traced here: 497 us
  local copies, waits for them, and re-layouts  185 us (37%)
  matrix products  93.3 us (18%)
  blocking collectives  84.8 us (17%)
  other arithmetic  74.4 us (15%)
  starting transfers between devices  42.1 us (8%)
  waiting for transfers between devices  14.2 us (3%)
    another operation x20, local copies, waits for them, and re-layouts, monomials(): jnp.stack([constant, across, upward, square_a, mixed, square_b, square_a...  102 us
    psum x1, blocking collectives, global_dot(): return lax.psum(value, ('sec', 'reg'))  84.8 us
    dot_general x10, matrix products, block_terms(): jnp.einsum('mpk,cpk->cmp', basis_a, mismatch, precision=FULL_PRECISION)  34.1 us
    dot_general x10, matrix products, block_terms(): jnp.einsum('mpk,cmp->cpk', basis_a, own, precision=FULL_PRECISION)  27.9 us
    scatter-add x4, other arithmetic, apply_normal(): products = products.at[:, first].add(to_own).at[:, second].add(to_other)  25 us
    ppermute x8, starting transfers between devices, shifted(): return lax.ppermute(array, axis, pairs)  23.6 us
    mul x10, other arithmetic, monomials(): square_b * upward  19.2 us
    dot_general x10, matrix products, block_terms(): jnp.einsum('mpk,cpk->cmp', basis_b, mismatch, precision=FULL_PRECISION)  18.3 us
  transfers between devices with their start and end apart: 16, of which 5 were waited for; matrix products, arithmetic and copies ran while one was open for 2% of the time, Pallas kernels for 0%

commit v1 on v0

--- a/solution.py
+++ b/solution.py
@@ -136,7 +136,10 @@
 
 
 def global_dot(value):
-    return lax.psum(value, ("sec", "reg"))
+    create_set = lambda local_values, comm_axis, link_axis: lax.psum(
+        lax.psum(local_values, axis_name=comm_axis), axis_name=link_axis
+    )
+    return create_set(value, "sec", "reg")
 
 
 def on_device(

time: 506 us -> 559 us (1.10)
  the two profiles are of different devices: /device:TPU:1 before, /device:TPU:2 now
where the time goes in v1:
time: 559 us; the launch traced here: 550 us
  local copies, waits for them, and re-layouts  185 us (33%)
  blocking collectives  142 us (25%)
  matrix products  93.3 us (17%)
  other arithmetic  74.5 us (13%)
  starting transfers between devices  42.6 us (8%)
  waiting for transfers between devices  9.47 us (2%)
    psum x1, blocking collectives, global_dot(): lax.psum(local_values, axis_name=comm_axis)  132 us
    another operation x20, local copies, waits for them, and re-layouts, monomials(): jnp.stack([constant, across, upward, square_a, mixed, square_b, square_a...  102 us
    dot_general x10, matrix products, block_terms(): jnp.einsum('mpk,cpk->cmp', basis_a, mismatch, precision=FULL_PRECISION)  34.1 us
    dot_general x10, matrix products, block_terms(): jnp.einsum('mpk,cmp->cpk', basis_a, own, precision=FULL_PRECISION)  27.9 us
    scatter-add x4, other arithmetic, apply_normal(): products = products.at[:, first].add(to_own).at[:, second].add(to_other)  25 us
    ppermute x8, starting transfers between devices, shifted(): return lax.ppermute(array, axis, pairs)  19.3 us
    mul x10, other arithmetic, monomials(): square_b * upward  19.3 us
    dot_general x10, matrix products, block_terms(): jnp.einsum('mpk,cpk->cmp', basis_b, mismatch, precision=FULL_PRECISION)  18.3 us
  transfers between devices with their start and end apart: 16, of which 5 were waited for; matrix products, arithmetic and copies ran while one was open for 2% of the time, Pallas kernels for 0%

profile of v1, /device:TPU:2, one launch (start us, length us, event | category | flops | bytes accessed | tf_op | source)
XLA Modules:
  0.0 549.9 jit_solution(1911731957454355684)
XLA Ops:
  4.6 3.4 collective-permute-start.2
  8.7 2.4 collective-permute-start.3
  12.4 3.5 collective-permute-start.1
  22.6 152.0 %while.24 = (s32[]{:T(128)}, f32[5,20,128]{2,1,0:T(8,128)}, f32[5,20,128]{2,1,0:T(8,128)}, s32[5,128]{1,0:T(8,128)S(1)}, f32[20,416]{0,1:T(8,128)}, /*index=5*/b...) while((s32[]{:T(128)}, f32[5,20,128]{2,1,0:T(8,128)}, ...), condition=%wide.region_1.4_spmd, body=%wide.region_0.3_spmd.sunk | while | flops 32287744 | bytes 16952436 | solution.py:128
  23.6 1.9 multiply_multiply_fusion.20
  26.8 4.8 stack.53
  32.4 5.4 stack.52
  39.6 2.8 fusion.96
  48.9 3.4 convolution_bitcast_fusion.4
  57.2 4.8 stack.53
  62.8 5.4 stack.52
  70.0 2.8 fusion.96
  79.3 3.4 convolution_bitcast_fusion.4
  87.6 4.8 stack.53
  93.2 5.4 stack.52
  100.4 2.8 fusion.96
  109.7 3.4 convolution_bitcast_fusion.4
  118.0 4.8 stack.53
  123.5 5.4 stack.52
  130.8 2.8 fusion.96
  140.1 3.4 convolution_bitcast_fusion.4
  145.2 1.9 multiply_multiply_fusion.20
  148.3 4.8 stack.53
  153.9 5.4 stack.52
  161.2 2.8 fusion.96
  170.5 3.4 convolution_bitcast_fusion.4
  176.8 6.4 %scatter_custom_fusion = f32[20,416]{0,1:T(8,128)S(1)} fusion(s32[640]{0:T(1024)} %fusion.40, f32[640,20]{1,0:T(8,128)S(1)} %copy.78, f32[]{:T(128)} %constant.56.clone.1), kind=kCustom, calls=%fused_computation.104 | custom fusion | flops 12800 | bytes 33792 | tf_op jit(solution)/shard_map/scatter-add | solution.py:134
  183.2 6.1 %scatter_fusion = f32[20,416]{0,1:T(8,128)S(1)} fusion(f32[20,416]{0,1:T(8,128)S(1)} %scatter_custom_fusion, s32[640]{0:T(1024)S(1)} %fusion.41, f32[640,20]{1,0:T(8,128)S(1)} %copy.80), kind=kCustom, calls=%fused_computation.9 | custom fusion | flops 12800 | bytes 156160 | tf_op jit(solution)/shard_map/scatter-add | solution.py:134
  193.9 3.4 collective-permute-start.6
  197.3 2.4 collective-permute-start.7
  200.5 2.3 collective-permute-done.7
  203.5 4.0 collective-permute-start.8
  208.9 3.1 collective-permute-start.10
  212.0 4.8 collective-permute-start.9
  216.9 2.7 collective-permute-start.11
  219.8 2.6 collective-permute-done.11
  224.9 152.0 %while.25 = (s32[]{:T(128)}, f32[5,20,128]{2,1,0:T(8,128)}, f32[5,20,128]{2,1,0:T(8,128)}, s32[5,128]{1,0:T(8,128)S(1)}, f32[20,416]{0,1:T(8,128)}, /*index=5*/b...) while((s32[]{:T(128)}, f32[5,20,128]{2,1,0:T(8,128)}, ...), condition=%wide.region_10.13_spmd, body=%wide.region_9.12_spmd.sunk | while | flops 32287744 | bytes 16952436 | solution.py:128
  229.1 4.8 stack.71
  234.7 5.4 stack.70
  242.0 2.8 fusion.109
  251.2 3.4 convolution_bitcast_fusion.5
  256.3 1.9 multiply_multiply_fusion.22
  259.5 4.8 stack.71
  265.1 5.4 stack.70
  272.3 2.8 fusion.109
  281.6 3.4 convolution_bitcast_fusion.5
  289.9 4.8 stack.71
  295.5 5.4 stack.70
  302.7 2.8 fusion.109
  312.0 3.4 convolution_bitcast_fusion.5
  320.3 4.8 stack.71
  325.9 5.4 stack.70
  333.1 2.8 fusion.109
  342.4 3.4 convolution_bitcast_fusion.5
  350.7 4.8 stack.71
  356.3 5.4 stack.70
  363.5 2.8 fusion.109
  372.8 3.4 convolution_bitcast_fusion.5
  379.1 6.4 %scatter_custom_fusion.4 = f32[20,416]{0,1:T(8,128)S(1)} fusion(s32[640]{0:T(1024)} %fusion.40, f32[640,20]{1,0:T(8,128)S(1)} %copy.89, f32[]{:T(128)} %constant.56.clone.1), kind=kCustom, calls=%fused_computation.102 | custom fusion | flops 12800 | bytes 33792 | tf_op jit(solution)/shard_map/scatter-add | solution.py:134
  385.5 6.1 %scatter_fusion.1 = f32[20,416]{0,1:T(8,128)S(1)} fusion(f32[20,416]{0,1:T(8,128)S(1)} %scatter_custom_fusion.4, s32[640]{0:T(1024)S(1)} %fusion.41, f32[640,20]{1,0:T(8,128)S(1)} %copy.91), kind=kCustom, calls=%fused_computation.13 | custom fusion | flops 12800 | bytes 156160 | tf_op jit(solution)/shard_map/scatter-add | solution.py:134
  396.1 2.2 collective-permute-start.14
  398.3 3.6 collective-permute-start.15
  405.3 131.9 %all-reduce = (f32[]{:T(128)}, f32[]{:T(128)}) all-reduce(f32[]{:T(128)} %get-tuple-element.119, f32[]{:T(128)} %get-tuple-element.118), channel_id=1, replica_groups=mesh['sec'=64,'reg'=4] {'sec'}, use_global_device_ids=true, to_apply=%region_7.10 | all-reduce | flops 2 | bytes 16 | tf_op jit(solution)/shard_map/psum | solution.py:140
  537.2 10.0 %all-reduce.1 = (f32[]{:T(128)}, f32[]{:T(128)}) all-reduce(f32[]{:T(128)} %get-tuple-element.152, f32[]{:T(128)} %get-tuple-element.153), channel_id=1, replica_groups=mesh['sec'=64,'reg'=4] {'reg'}, use_global_device_ids=true, to_apply=%region_8.11 | all-reduce | flops 2 | bytes 16 | tf_op jit(solution)/shard_map/psum | solution.py:139
  (361 shorter events, 168.6 us)
Async XLA Ops:
  1.4 21.2 %copy-start.2 = (f32[1,1,20,128]{2,3,1,0:T(8,128)}, f32[1,1,20,128]{2,3,1,0:T(8,128)S(1)}, u32[]{:S(2)}) copy-start(f32[1,1,20,128]{2,3,1,0:T(8,128)S(1)} %copy.69) | copy-start | bytes 30724
  1.4 11.0 %collective-permute-start = (f32[20,128]{0,1:T(8,128)S(1)}, f32[20,128]{0,1:T(8,128)S(1)}, u32[]{:S(2)}, u32[]{:S(2)}) collective-permute-start(f32[20,128]{0,1:T(8,128)S(1)} %bitcast.359), channel_id=1, source_target_pairs={{0,4},{4,8},{8,12},{12,16},{16,20},{20,24},{24,28},{28,32},{32,36}... | collective-permute-start | bytes 30728 | tf_op jit(solution)/shard_map/ppermute | solution.py:13
  4.0 4.1 copy-start.12
  4.0 16.1 %copy-start.10 = (pred[16]{0:T(512)(128)(4,1)}, pred[16]{0:T(512)(128)(4,1)S(1)}, u32[]{:S(2)}) copy-start(pred[16]{0:T(512)(128)(4,1)S(1)} %get-tuple-element.164) | copy-start | bytes 52
  4.6 15.4 %collective-permute-start.2 = (f32[1,20,16]{1,2,0:T(8,128)S(1)}, f32[1,20,16]{1,2,0:T(8,128)S(1)}, u32[]{:S(2)}, u32[]{:S(2)}) collective-permute-start(f32[1,20,16]{1,2,0:T(8,128)S(1)} %select_bitcast_fusion.7), channel_id=1, source_target_pairs={{0,1},{1,2},{2,3},{4,5},{5,6},{6,7},{8,9},{9,10},{10,11},{12,13},{... | collective-permute-start | bytes 3848 | tf_op jit(solution)/shard_map/ppermute | solution.py:23
  8.0 12.1 %copy-start.9 = (s32[1024]{0:T(1024)}, s32[1024]{0:T(1024)S(1)}, u32[]{:S(2)}) copy-start(s32[1024]{0:T(1024)S(1)} %pad_clamp_fusion.4) | copy-start | bytes 12292
  8.7 11.5 %collective-permute-start.3 = (f32[1,20,16]{1,2,0:T(8,128)S(1)}, f32[1,20,16]{1,2,0:T(8,128)S(1)}, u32[]{:S(2)}, u32[]{:S(2)}) collective-permute-start(f32[1,20,16]{1,2,0:T(8,128)S(1)} %select_bitcast_fusion.6), channel_id=1, source_target_pairs={{1,0},{2,1},{3,2},{5,4},{6,5},{7,6},{9,8},{10,9},{11,10},{13,12},{... | collective-permute-start | bytes 3848 | tf_op jit(solution)/shard_map/ppermute | solution.py:24
  12.4 7.9 %collective-permute-start.1 = (f32[20,128]{0,1:T(8,128)S(1)}, f32[20,128]{0,1:T(8,128)S(1)}, u32[]{:S(2)}, u32[]{:S(2)}) collective-permute-start(f32[20,128]{0,1:T(8,128)S(1)} %collective-permute-done), channel_id=1, source_target_pairs={{0,4},{4,8},{8,12},{12,16},{16,20},{20,24},{24,28},{28,32},{32,36}... | collective-permute-start | bytes 30728 | tf_op jit(solution)/shard_map/ppermute | solution.py:13
  174.6 16.0 %copy-start.14 = (s32[1,1,2,16]{3,2,1,0:T(2,128)S(1)}, s32[1,1,2,16]{3,2,1,0:T(2,128)}, u32[]{:S(2)}) copy-start(s32[1,1,2,16]{3,2,1,0:T(2,128)} %param.23) | copy-start | bytes 388
  174.6 16.0 %copy-start.7 = (f32[1,1,20,128]{3,1,2,0:T(1,128)S(1)}, f32[1,1,20,128]{3,1,2,0:T(1,128)}, u32[]{:S(2)}) copy-start(f32[1,1,20,128]{3,1,2,0:T(1,128)} %param.18) | copy-start | bytes 30724
  174.6 16.2 %copy-start.8 = (f32[1,1,20,128]{3,1,2,0:T(1,128)S(1)}, f32[1,1,20,128]{3,1,2,0:T(1,128)}, u32[]{:S(2)}) copy-start(f32[1,1,20,128]{3,1,2,0:T(1,128)} %param.17) | copy-start | bytes 30724
  174.6 25.1 %copy-start.3 = (f32[1,1,20,128]{2,3,1,0:T(8,128)S(1)}, f32[1,1,20,128]{2,3,1,0:T(8,128)}, u32[]{:S(2)}) copy-start(f32[1,1,20,128]{2,3,1,0:T(8,128)} %copy-done.2) | copy-start | bytes 30724
  175.5 32.7 %copy-start.13 = (pred[16]{0:T(512)(128)(4,1)S(1)}, pred[16]{0:T(512)(128)(4,1)}, u32[]{:S(2)}) copy-start(pred[16]{0:T(512)(128)(4,1)} %copy-done.12) | copy-start | bytes 52
  175.5 41.3 %copy-start.11 = (pred[16]{0:T(512)(128)(4,1)S(1)}, pred[16]{0:T(512)(128)(4,1)}, u32[]{:S(2)}) copy-start(pred[16]{0:T(512)(128)(4,1)} %copy-done.10) | copy-start | bytes 52
  189.3 3.2 collective-permute-start.4
  190.6 34.3 %copy-start.15 = (s32[16]{0:T(128)}, s32[16]{0:T(128)S(1)}, u32[]{:S(2)}) copy-start(s32[16]{0:T(128)S(1)} %get-tuple-element.212) | copy-start | bytes 196
  190.7 34.2 %copy-start.16 = (s32[16]{0:T(128)}, s32[16]{0:T(128)S(1)}, u32[]{:S(2)}) copy-start(s32[16]{0:T(128)S(1)} %get-tuple-element.213) | copy-start | bytes 196
  190.8 34.1 %copy-start.5 = (f32[1,1,20,128]{2,3,1,0:T(8,128)}, f32[1,1,20,128]{2,3,1,0:T(8,128)S(1)}, u32[]{:S(2)}) copy-start(f32[1,1,20,128]{2,3,1,0:T(8,128)S(1)} %copy.81) | copy-start | bytes 30724
  192.6 7.2 %collective-permute-start.5 = (f32[20,128]{0,1:T(8,128)S(1)}, f32[20,128]{0,1:T(8,128)S(1)}, u32[]{:S(2)}, u32[]{:S(2)}) collective-permute-start(f32[20,128]{0,1:T(8,128)S(1)} %slice_add_fusion.2), channel_id=1, source_target_pairs={{4,0},{8,4},{12,8},{16,12},{20,16},{24,20},{28,24},{32,28},{36,32}... | collective-permute-start | bytes 30728 | tf_op jit(solution)/shard_map/ppermute | solution.py:13
  193.9 5.9 %collective-permute-start.6 = (f32[1,20,16]{1,2,0:T(8,128)S(1)}, f32[1,20,16]{1,2,0:T(8,128)S(1)}, u32[]{:S(2)}, u32[]{:S(2)}) collective-permute-start(f32[1,20,16]{1,2,0:T(8,128)S(1)} %get-tuple-element.209), channel_id=1, source_target_pairs={{0,1},{1,2},{2,3},{4,5},{5,6},{6,7},{8,9},{9,10},{10,11},{12,13},{... | collective-permute-start | bytes 3848 | tf_op jit(solution)/shard_map/ppermute | solution.py:23
  197.3 5.5 %collective-permute-start.7 = (f32[1,20,16]{1,2,0:T(8,128)S(1)}, f32[1,20,16]{1,2,0:T(8,128)S(1)}, u32[]{:S(2)}, u32[]{:S(2)}) collective-permute-start(f32[1,20,16]{1,2,0:T(8,128)S(1)} %get-tuple-element.208), channel_id=1, source_target_pairs={{1,0},{2,1},{3,2},{5,4},{6,5},{7,6},{9,8},{10,9},{11,10},{13,12},{... | collective-permute-start | bytes 3848 | tf_op jit(solution)/shard_map/ppermute | solution.py:24
  203.5 21.4 %copy-start = (f32[20,128]{0,1:T(8,128)}, f32[20,128]{0,1:T(8,128)S(1)}, u32[]{:S(2)}) copy-start(f32[20,128]{0,1:T(8,128)S(1)} %bitcast_subtract_fusion) | copy-start | bytes 30724
  203.5 8.5 %collective-permute-start.8 = (f32[20,128]{0,1:T(8,128)S(1)}, f32[20,128]{0,1:T(8,128)S(1)}, u32[]{:S(2)}, u32[]{:S(2)}) collective-permute-start(f32[20,128]{0,1:T(8,128)S(1)} %bitcast_subtract_fusion), channel_id=1, source_target_pairs={{0,4},{4,8},{8,12},{12,16},{16,20},{20,24},{24,28},{28,32},{32,36}... | collective-permute-start | bytes 30728 | tf_op jit(solution)/shard_map/ppermute | solution.py:13
  208.9 10.8 %collective-permute-start.10 = (f32[1,20,16]{1,2,0:T(8,128)S(1)}, f32[1,20,16]{1,2,0:T(8,128)S(1)}, u32[]{:S(2)}, u32[]{:S(2)}) collective-permute-start(f32[1,20,16]{1,2,0:T(8,128)S(1)} %select_bitcast_fusion.5), channel_id=1, source_target_pairs={{0,1},{1,2},{2,3},{4,5},{5,6},{6,7},{8,9},{9,10},{10,11},{12,13},{... | collective-permute-start | bytes 3848 | tf_op jit(solution)/shard_map/ppermute | solution.py:23
  212.0 10.6 %collective-permute-start.9 = (f32[20,128]{0,1:T(8,128)S(1)}, f32[20,128]{0,1:T(8,128)S(1)}, u32[]{:S(2)}, u32[]{:S(2)}) collective-permute-start(f32[20,128]{0,1:T(8,128)S(1)} %collective-permute-done.8), channel_id=1, source_target_pairs={{0,4},{4,8},{8,12},{12,16},{16,20},{20,24},{24,28},{28,32},{32,36}... | collective-permute-start | bytes 30728 | tf_op jit(solution)/shard_map/ppermute | solution.py:13
  216.9 5.5 %collective-permute-start.11 = (f32[1,20,16]{1,2,0:T(8,128)S(1)}, f32[1,20,16]{1,2,0:T(8,128)S(1)}, u32[]{:S(2)}, u32[]{:S(2)}) collective-permute-start(f32[1,20,16]{1,2,0:T(8,128)S(1)} %select_bitcast_fusion.4), channel_id=1, source_target_pairs={{1,0},{2,1},{3,2},{5,4},{6,5},{7,6},{9,8},{10,9},{11,10},{13,12},{... | collective-permute-start | bytes 3848 | tf_op jit(solution)/shard_map/ppermute | solution.py:24
  376.9 25.1 %copy-start.1 = (f32[20,128]{0,1:T(8,128)S(1)}, f32[20,128]{0,1:T(8,128)}, u32[]{:S(2)}) copy-start(f32[20,128]{0,1:T(8,128)} %copy-done) | copy-start | bytes 30724
  376.9 25.1 %copy-start.6 = (f32[1,1,20,128]{2,3,1,0:T(8,128)S(1)}, f32[1,1,20,128]{2,3,1,0:T(8,128)}, u32[]{:S(2)}) copy-start(f32[1,1,20,128]{2,3,1,0:T(8,128)} %copy-done.5) | copy-start | bytes 30724
  376.9 171.6 %copy-start.4 = (f32[1,1,20,128]{2,3,1,0:T(8,128)S(1)}, f32[1,1,20,128]{2,3,1,0:T(8,128)}, u32[]{:S(2)}) copy-start(f32[1,1,20,128]{2,3,1,0:T(8,128)} %copy-done.2) | copy-start | bytes 30724
  391.6 3.1 collective-permute-start.12
  394.8 7.2 %collective-permute-start.13 = (f32[20,128]{0,1:T(8,128)S(1)}, f32[20,128]{0,1:T(8,128)S(1)}, u32[]{:S(2)}, u32[]{:S(2)}) collective-permute-start(f32[20,128]{0,1:T(8,128)S(1)} %slice_add_fusion), channel_id=1, source_target_pairs={{4,0},{8,4},{12,8},{16,12},{20,16},{24,20},{28,24},{32,28},{36,32}... | collective-permute-start | bytes 30728 | tf_op jit(solution)/shard_map/ppermute | solution.py:13
  396.1 5.9 %collective-permute-start.14 = (f32[1,20,16]{1,2,0:T(8,128)S(1)}, f32[1,20,16]{1,2,0:T(8,128)S(1)}, u32[]{:S(2)}, u32[]{:S(2)}) collective-permute-start(f32[1,20,16]{1,2,0:T(8,128)S(1)} %get-tuple-element.207), channel_id=1, source_target_pairs={{0,1},{1,2},{2,3},{4,5},{5,6},{6,7},{8,9},{9,10},{10,11},{12,13},{... | collective-permute-start | bytes 3848 | tf_op jit(solution)/shard_map/ppermute | solution.py:23
  398.3 5.5 %collective-permute-start.15 = (f32[1,20,16]{1,2,0:T(8,128)S(1)}, f32[1,20,16]{1,2,0:T(8,128)S(1)}, u32[]{:S(2)}, u32[]{:S(2)}) collective-permute-start(f32[1,20,16]{1,2,0:T(8,128)S(1)} %get-tuple-element.206), channel_id=1, source_target_pairs={{1,0},{2,1},{3,2},{5,4},{6,5},{7,6},{9,8},{10,9},{11,10},{13,12},{... | collective-permute-start | bytes 3848 | tf_op jit(solution)/shard_map/ppermute | solution.py:24
